TPU v7x, 32 devices: a whole 2x2x4 slice. The times are simulated.
32 devices in a mesh: gx: 4 (over z), gy: 2 (over x), gz: 4 (over y, core).
Axes of the slice: x: 2, y: 2, z: 4, core: 2. Of those that a mesh axis runs over, the one named last changes fastest.
Arguments:
- queries: bfloat16 [64, 1024, 512], P(('gx', 'gy'), 'gz'), may hold values from -48 to 48
- key_vectors: bfloat16 [64, 1024, 128], P(('gx', 'gy'), 'gz'), may hold values from -12 to 12
- value_vectors: bfloat16 [64, 1024, 128], P(('gx', 'gy'), 'gz'), may hold values from -6 to 6
- chosen: int32 [64, 2], P(('gx', 'gy')), may hold values from -1 to 63, as said below
Outputs:
- attended: bfloat16 [64, 1024, 512], P(('gx', 'gy'), 'gz')
Inputs may be any that keep to these rules, and one draw needn't show every extreme that they name: `chosen`: both entries of a row are -1, or both are blocks of two different groups before the row's own group, counting blocks in groups of 8 consecutive blocks. One group's rows name blocks of any one group in at most 1 entries; every group from the third on names blocks of the first group in exactly 1 entries. The rows of the first two groups are all -1.
All inputs are finite; a program needn't handle non-finite values.
Results may differ from a plain program's by a relative error of at most 0.0042.
Values may be sent and summed in bfloat16 or wider, within the bound.
No kernel may reach another device: no remote copies, remote signals or barrier semaphores. Data moves between devices by JAX's collectives and lax.ppermute only.
A program may use at most 128 MiB of HBM per device.

v0:
```python
import jax
import jax.numpy as jnp
from jax import lax
from jax.sharding import PartitionSpec as P

CAP = 1


def allowed_mask(token_start, query_count, head_count, block_len, live_pair):
    token_pos = token_start + jnp.arange(query_count * head_count, dtype=jnp.int32) // head_count
    key_pos = jnp.arange(3 * block_len, dtype=jnp.int32)
    own_part = (key_pos[None, :] < block_len) & (key_pos[None, :] <= token_pos[:, None])
    pair_slot = jnp.clip(key_pos // block_len - 1, 0, 1)
    far_part = (key_pos >= block_len) & (live_pair[pair_slot] > 0)
    return own_part | far_part[None, :]


def attend_block(query_block, key_sets, value_sets, allowed):
    head_dim = key_sets.shape[1]
    flat_queries = query_block.reshape(-1, head_dim)
    scores = jnp.dot(flat_queries, key_sets.T, preferred_element_type=jnp.float32) * head_dim ** (
        -0.5
    )
    scores = jnp.where(allowed, scores, -jnp.inf)
    row_top = jnp.max(scores, axis=1, keepdims=True)
    weights = jnp.exp(scores - row_top)
    row_total = jnp.sum(weights, axis=1, keepdims=True)
    mixed = (
        jnp.dot(weights.astype(jnp.bfloat16), value_sets, preferred_element_type=jnp.float32)
        / row_total
    )
    return mixed.astype(jnp.bfloat16).reshape(query_block.shape)


def body(queries, key_vectors, value_vectors, chosen):
    blocks_here, quarter, row_width = queries.shape
    head_dim = key_vectors.shape[2]
    head_count = row_width // head_dim
    groups = lax.axis_size(("gx", "gy"))
    quarter_index = lax.axis_index("gz")
    entries = chosen.reshape(-1)
    entry_count = entries.shape[0]
    live_entry = entries >= 0
    owner_group = jnp.where(live_entry, entries // blocks_here, -1)
    local_block = jnp.where(live_entry, entries % blocks_here, 0)
    entry_ids = jnp.arange(entry_count, dtype=jnp.int32)
    same_owner = (owner_group[:, None] == owner_group[None, :]) & live_entry[None, :]
    slot_rank = jnp.sum(same_owner & (entry_ids[None, :] < entry_ids[:, None]), axis=1)
    group_ids = jnp.arange(groups, dtype=jnp.int32)
    slot_ids = jnp.arange(CAP, dtype=jnp.int32)
    hits = (owner_group[:, None, None] == group_ids[None, :, None]) & (
        slot_rank[:, None, None] == slot_ids[None, None, :]
    )
    want_table = jnp.sum(jnp.where(hits, local_block[:, None, None] + 1, 0), axis=0)
    requests = lax.all_to_all(want_table, ("gx", "gy"), split_axis=0, concat_axis=0, tiled=True)
    paired = jnp.concatenate([key_vectors, value_vectors], axis=2)
    wanted = jnp.maximum(requests - 1, 0).reshape(-1)
    outgoing = jnp.take(paired, wanted, axis=0).reshape(groups, CAP, quarter, 2 * head_dim)
    incoming = lax.all_to_all(outgoing, ("gx", "gy"), split_axis=0, concat_axis=0, tiled=True)
    incoming = incoming.reshape(groups * CAP, quarter, 2 * head_dim)
    flat_slot = jnp.maximum(owner_group, 0) * CAP + jnp.minimum(slot_rank, CAP - 1)
    fetched = jnp.take(incoming, flat_slot, axis=0)
    fetched_full, own_blocks = (
        lax.all_gather(fetched, "gz", axis=1, tiled=True),
        lax.all_gather(paired, "gz", axis=1, tiled=True),
    )
    block_len = fetched_full.shape[1]
    pair_blocks = fetched_full.reshape(blocks_here, 2, block_len, 2 * head_dim)
    live_pairs = live_entry.astype(jnp.int32).reshape(blocks_here, 2)

    def one_block(operands):
        query_block, own_pair, far_pair, live_pair = operands
        key_sets = jnp.concatenate(
            [own_pair[:, :head_dim], far_pair[0, :, :head_dim], far_pair[1, :, :head_dim]], axis=0
        )
        value_sets = jnp.concatenate(
            [own_pair[:, head_dim:], far_pair[0, :, head_dim:], far_pair[1, :, head_dim:]], axis=0
        )
        allowed = allowed_mask(quarter_index * quarter, quarter, head_count, block_len, live_pair)
        return attend_block(query_block, key_sets, value_sets, allowed)

    return lax.map(one_block, (queries, own_blocks, pair_blocks, live_pairs))


def solution(mesh):
    placed = (
        P(("gx", "gy"), "gz", None),
        P(("gx", "gy"), "gz", None),
        P(("gx", "gy"), "gz", None),
        P(("gx", "gy"), None),
    )
    return jax.shard_map(
        body, mesh=mesh, in_specs=placed, out_specs=P(("gx", "gy"), "gz", None), check_vma=False
    )
```

profile of v0, /device:TPU:0, one launch (start us, length us, event | category | flops | bytes accessed | tf_op | source)
XLA Modules:
  0.0 239.3 jit_solution(9529049361917233739)
XLA Ops:
  7.7 1.2 constant_dynamic-update-slice_fusion.1
  10.5 13.6 %all_to_all.14 = s32[8,1,1]{2,1,0:T(1,128)S(1)} all-to-all(s32[8,1,1]{2,1,0:T(1,128)S(1)} %copy.16), channel_id=1, replica_groups=mesh['gx'=4,'gy'=2,'gz'=4] {'gx','gy'}, dimensions={0} | all-to-all | bytes 64 | tf_op jit(solution)/shard_map/all_to_all | solution.py:55
  24.3 1.8 gather_fusion
  27.5 3.6 %all-to-all-start.1 = ((bf16[8,1,256,256]{3,2,1,0:T(8,128)(2,1)}), bf16[8,1,256,256]{3,2,1,0:T(8,128)(2,1)S(1)}, u32[]{:S(2)}, u32[]{:S(2)}) async-start(bf16[8,1,256,256]{3,2,1,0:T(8,128)(2,1)} %bitcast_select_fusion), calls=%async_computation.1 | async-start | bytes 2097152 | tf_op jit(solution)/shard_map/all_to_all | solution.py:59
  31.2 24.6 %all-to-all-done.1 = bf16[8,1,256,256]{3,2,1,0:T(8,128)(2,1)S(1)} async-done(((bf16[8,1,256,256]{3,2,1,0:T(8,128)(2,1)}), bf16[8,1,256,256]{3,2,1,0:T(8,128)(2,1)S(1)}, u32[]{:S(2)}, u32[]{:S(2)}) %all-to-all-start.1) | async-done | bytes 1048608 | tf_op jit(solution)/shard_map/all_to_all | solution.py:59
  56.5 1.6 broadcast_select_fusion
  58.2 57.3 %all-gather.5.cloned.1.call-done = bf16[16,1024,256]{2,1,0:T(8,128)(2,1)} async-done(((bf16[16,256,256]{2,1,0:T(8,128)(2,1)}), bf16[16,1024,256]{2,1,0:T(8,128)(2,1)}) %all-gather.5.cloned.1.call-update) | async-done | bytes 8388624 | tf_op jit(solution)/shard_map/all_gather | solution.py:64
  115.5 117.0 %while.13 = (s32[]{:T(128)}, bf16[8,256,512]{2,1,0:T(8,128)(2,1)}, s32[]{:T(128)}, s32[8,2]{0,1:T(2,128)S(1)}, bf16[8,256,512]{2,1,0:T(8,128)(2,1)}, /*index=5*/...) while((s32[]{:T(128)}, bf16[8,256,512]{2,1,0:T(8,128)(2,1)}, s32[]{:T(128)}, ...), condition=%wide.region_5.6_spmd, body=%wide.region_2.5_spmd.sunk | while | flops 1647116288 | bytes 48282256 | solution.py:82
  116.1 1.3 compare_reduce_fusion.3
  117.5 1.3 dynamic-slice_bitcast_fusion.4
  121.2 4.1 %fusion.58 = (f32[1024]{0:T(1024)S(1)}, f32[1024,3072]{1,0:T(8,128)S(1)}) fusion(bf16[1024,128]{1,0:T(8,128)(2,1)S(1)} %reshape.508, bf16[1024,128]{1,0:T(8,128)(2,1)S(1)} %get-tuple-element.211, bf16[1024,128]{1,0:T(8,128)(2,1)S(1)} %get-tuple-element.212, bf16[1024,128]{1,0:T(8,128)(2,1)S(1)} %get-tuple-element.213, ...), kind=kOutput, calls=%fused_computation.92.clone.1 | convolution fusion | flops 826539008 | bytes 13645824 | tf_op jit(solution)/shard_map/while/body/eval_jaxpr/dot_general | solution.py:21
  125.3 1.9 fusion.59
  127.2 2.0 fusion.60
  130.8 1.3 compare_reduce_fusion.3
  132.1 1.3 dynamic-slice_bitcast_fusion.4
  135.9 4.1 %fusion.58 = (f32[1024]{0:T(1024)S(1)}, f32[1024,3072]{1,0:T(8,128)S(1)}) fusion(bf16[1024,128]{1,0:T(8,128)(2,1)S(1)} %reshape.508, bf16[1024,128]{1,0:T(8,128)(2,1)S(1)} %get-tuple-element.211, bf16[1024,128]{1,0:T(8,128)(2,1)S(1)} %get-tuple-element.212, bf16[1024,128]{1,0:T(8,128)(2,1)S(1)} %get-tuple-element.213, ...), kind=kOutput, calls=%fused_computation.92.clone.1 | convolution fusion | flops 826539008 | bytes 13645824 | tf_op jit(solution)/shard_map/while/body/eval_jaxpr/dot_general | solution.py:21
  140.0 1.9 fusion.59
  141.8 2.0 fusion.60
  145.4 1.3 compare_reduce_fusion.3
  146.7 1.3 dynamic-slice_bitcast_fusion.4
  150.5 4.1 %fusion.58 = (f32[1024]{0:T(1024)S(1)}, f32[1024,3072]{1,0:T(8,128)S(1)}) fusion(bf16[1024,128]{1,0:T(8,128)(2,1)S(1)} %reshape.508, bf16[1024,128]{1,0:T(8,128)(2,1)S(1)} %get-tuple-element.211, bf16[1024,128]{1,0:T(8,128)(2,1)S(1)} %get-tuple-element.212, bf16[1024,128]{1,0:T(8,128)(2,1)S(1)} %get-tuple-element.213, ...), kind=kOutput, calls=%fused_computation.92.clone.1 | convolution fusion | flops 826539008 | bytes 13645824 | tf_op jit(solution)/shard_map/while/body/eval_jaxpr/dot_general | solution.py:21
  154.6 1.9 fusion.59
  156.4 2.0 fusion.60
  160.0 1.3 compare_reduce_fusion.3
  161.3 1.3 dynamic-slice_bitcast_fusion.4
  165.1 4.1 %fusion.58 = (f32[1024]{0:T(1024)S(1)}, f32[1024,3072]{1,0:T(8,128)S(1)}) fusion(bf16[1024,128]{1,0:T(8,128)(2,1)S(1)} %reshape.508, bf16[1024,128]{1,0:T(8,128)(2,1)S(1)} %get-tuple-element.211, bf16[1024,128]{1,0:T(8,128)(2,1)S(1)} %get-tuple-element.212, bf16[1024,128]{1,0:T(8,128)(2,1)S(1)} %get-tuple-element.213, ...), kind=kOutput, calls=%fused_computation.92.clone.1 | convolution fusion | flops 826539008 | bytes 13645824 | tf_op jit(solution)/shard_map/while/body/eval_jaxpr/dot_general | solution.py:21
  169.2 1.9 fusion.59
  171.1 2.0 fusion.60
  174.6 1.3 compare_reduce_fusion.3
  175.9 1.3 dynamic-slice_bitcast_fusion.4
  179.7 4.1 %fusion.58 = (f32[1024]{0:T(1024)S(1)}, f32[1024,3072]{1,0:T(8,128)S(1)}) fusion(bf16[1024,128]{1,0:T(8,128)(2,1)S(1)} %reshape.508, bf16[1024,128]{1,0:T(8,128)(2,1)S(1)} %get-tuple-element.211, bf16[1024,128]{1,0:T(8,128)(2,1)S(1)} %get-tuple-element.212, bf16[1024,128]{1,0:T(8,128)(2,1)S(1)} %get-tuple-element.213, ...), kind=kOutput, calls=%fused_computation.92.clone.1 | convolution fusion | flops 826539008 | bytes 13645824 | tf_op jit(solution)/shard_map/while/body/eval_jaxpr/dot_general | solution.py:21
  183.8 1.9 fusion.59
  185.7 2.0 fusion.60
  189.2 1.3 compare_reduce_fusion.3
  190.6 1.3 dynamic-slice_bitcast_fusion.4
  194.3 4.1 %fusion.58 = (f32[1024]{0:T(1024)S(1)}, f32[1024,3072]{1,0:T(8,128)S(1)}) fusion(bf16[1024,128]{1,0:T(8,128)(2,1)S(1)} %reshape.508, bf16[1024,128]{1,0:T(8,128)(2,1)S(1)} %get-tuple-element.211, bf16[1024,128]{1,0:T(8,128)(2,1)S(1)} %get-tuple-element.212, bf16[1024,128]{1,0:T(8,128)(2,1)S(1)} %get-tuple-element.213, ...), kind=kOutput, calls=%fused_computation.92.clone.1 | convolution fusion | flops 826539008 | bytes 13645824 | tf_op jit(solution)/shard_map/while/body/eval_jaxpr/dot_general | solution.py:21
  198.4 1.9 fusion.59
  200.3 2.0 fusion.60
  203.9 1.3 compare_reduce_fusion.3
  205.2 1.3 dynamic-slice_bitcast_fusion.4
  209.0 4.1 %fusion.58 = (f32[1024]{0:T(1024)S(1)}, f32[1024,3072]{1,0:T(8,128)S(1)}) fusion(bf16[1024,128]{1,0:T(8,128)(2,1)S(1)} %reshape.508, bf16[1024,128]{1,0:T(8,128)(2,1)S(1)} %get-tuple-element.211, bf16[1024,128]{1,0:T(8,128)(2,1)S(1)} %get-tuple-element.212, bf16[1024,128]{1,0:T(8,128)(2,1)S(1)} %get-tuple-element.213, ...), kind=kOutput, calls=%fused_computation.92.clone.1 | convolution fusion | flops 826539008 | bytes 13645824 | tf_op jit(solution)/shard_map/while/body/eval_jaxpr/dot_general | solution.py:21
  213.0 1.9 fusion.59
  214.9 2.0 fusion.60
  218.5 1.3 compare_reduce_fusion.3
  219.8 1.3 dynamic-slice_bitcast_fusion.4
  223.6 4.1 %fusion.58 = (f32[1024]{0:T(1024)S(1)}, f32[1024,3072]{1,0:T(8,128)S(1)}) fusion(bf16[1024,128]{1,0:T(8,128)(2,1)S(1)} %reshape.508, bf16[1024,128]{1,0:T(8,128)(2,1)S(1)} %get-tuple-element.211, bf16[1024,128]{1,0:T(8,128)(2,1)S(1)} %get-tuple-element.212, bf16[1024,128]{1,0:T(8,128)(2,1)S(1)} %get-tuple-element.213, ...), kind=kOutput, calls=%fused_computation.92.clone.1 | convolution fusion | flops 826539008 | bytes 13645824 | tf_op jit(solution)/shard_map/while/body/eval_jaxpr/dot_general | solution.py:21
  227.7 1.9 fusion.59
  229.5 2.0 fusion.60
  (116 shorter events, 37.2 us)
Async XLA Ops:
  6.5 3.3 %copy-start.1 = (s32[8,2]{0,1:T(2,128)S(1)}, s32[8,2]{0,1:T(2,128)}, u32[]{:S(2)}) copy-start(s32[8,2]{0,1:T(2,128)} %param.9) | copy-start | bytes 196
  6.5 51.7 %all-gather.3.cloned.1.call-start = ((), (), s32[]{:S(2)}) async-start(), calls=%async_computation.2 | async-start | bytes 5242880 | tf_op jit(solution)/shard_map/all_gather | solution.py:65
  8.9 1.0 copy-start
  27.5 28.3 %all-to-all-start.1 = ((bf16[8,1,256,256]{3,2,1,0:T(8,128)(2,1)}), bf16[8,1,256,256]{3,2,1,0:T(8,128)(2,1)S(1)}, u32[]{:S(2)}, u32[]{:S(2)}) async-start(bf16[8,1,256,256]{3,2,1,0:T(8,128)(2,1)} %bitcast_select_fusion), calls=%async_computation.1 | async-start | bytes 2097152 | tf_op jit(solution)/shard_map/all_to_all | solution.py:59
  31.1 84.4 %all-gather.5.cloned.1.call-start = ((), (), s32[]{:S(2)}) async-start(), calls=%async_computation.3 | async-start | bytes 10485760 | tf_op jit(solution)/shard_map/all_gather | solution.py:64
Sparse Core Ops, SparseCore 0:
  10.0 37.1 all-gather.2
  58.3 57.1 all-gather.4
where the time goes:
time: 241 us; the launch traced here: 239 us
  waiting for transfers between devices  81.9 us (34%)
  matrix products  48.7 us (20%)
  local copies, waits for them, and re-layouts  48.4 us (20%)
  other arithmetic  29.1 us (12%)
  blocking collectives  13.6 us (6%)
  between operations  13.5 us (6%)
  starting transfers between devices  3.61 us (1%)
    all_gather x1, waiting for transfers between devices, body(): lax.all_gather(fetched, 'gz', axis=1, tiled=True)  57.3 us
    dot_general x8, matrix products, attend_block(): jnp.dot(flat_queries, key_sets.T, preferred_element_type=jnp.float32)  32.7 us
    all_to_all x1, waiting for transfers between devices, body(): lax.all_to_all(outgoing, ('gx', 'gy'), split_axis=0, concat_axis=0, tiled...  24.6 us
    squeeze x16, local copies, waits for them, and re-layouts, body(): return lax.map(one_block, (queries, own_blocks, pair_blocks, live_pairs))  19.1 us
    dot_general x8, matrix products, attend_block(): jnp.dot(weights.astype(jnp.bfloat16), value_sets, preferred_element_type=...  16.1 us
    reduce_sum x8, other arithmetic, attend_block(): row_total = jnp.sum(weights, axis=1, keepdims=True)  14.9 us
    all_to_all x1, blocking collectives, body(): lax.all_to_all(want_table, ('gx', 'gy'), split_axis=0, concat_axis=0, til...  13.6 us
    gt x8, other arithmetic, allowed_mask(): far_part = (key_pos >= block_len) & (live_pair[pair_slot] > 0)  10.5 us
  transfers between devices with their start and end apart: 3, of which 2 were waited for; matrix products, arithmetic and copies ran while one was open for 3% of the time, Pallas kernels for 0%

commit v1 on v0

--- a/solution.py
+++ b/solution.py
@@ -4,6 +4,28 @@
 from jax.sharding import PartitionSpec as P
 
 CAP = 1
+
+
+def split_up(x, dim, count):
+    before, after = (x.shape[:dim], x.shape[dim + 1 :])
+    return jnp.moveaxis(x.reshape(*before, count, -1, *after), dim, 0)
+
+
+def in_order(pieces, dim):
+    pieces = jnp.moveaxis(pieces, 0, dim)
+    shape = pieces.shape
+    return pieces.reshape(*shape[:dim], shape[dim] * shape[dim + 1], *shape[dim + 2 :])
+
+
+def pairwise_exchange(x, axis, split_dim, concat_dim):
+    size, here = (lax.axis_size(axis), lax.axis_index(axis))
+    pieces = split_up(x, split_dim, size)
+    finished = [pieces[here]]
+    for step in range(1, size):
+        sent = pieces[here ^ step]
+        finished.append(lax.ppermute(sent, axis, [(i, i ^ step) for i in range(size)]))
+    pieces = jnp.stack(finished)[here ^ jnp.arange(size)]
+    return in_order(pieces, concat_dim)
 
 
 def allowed_mask(token_start, query_count, head_count, block_len, live_pair):
@@ -52,7 +74,7 @@
         slot_rank[:, None, None] == slot_ids[None, None, :]
     )
     want_table = jnp.sum(jnp.where(hits, local_block[:, None, None] + 1, 0), axis=0)
-    requests = lax.all_to_all(want_table, ("gx", "gy"), split_axis=0, concat_axis=0, tiled=True)
+    requests = pairwise_exchange(want_table, ("gx", "gy"), 0, 0)
     paired = jnp.concatenate([key_vectors, value_vectors], axis=2)
     wanted = jnp.maximum(requests - 1, 0).reshape(-1)
     outgoing = jnp.take(paired, wanted, axis=0).reshape(groups, CAP, quarter, 2 * head_dim)

time: 241 us -> 250 us (1.037)
  blocking collectives: 13.6 us -> 0 us
  starting transfers between devices: 3.61 us -> 16.1 us
  local copies, waits for them, and re-layouts: 48.4 us -> 54.6 us
  waiting for transfers between devices: 81.9 us -> 86.8 us
    all_to_all x1 -> x0, blocking collectives: 13.6 us -> none  [body(): lax.all_to_all(want_table, ('gx', 'gy'), split_axis=0, concat_axis=0, til...]
    ppermute x0 -> x7, starting transfers between devices: none -> 12.5 us  [pairwise_exchange(): lax.ppermute(sent, axis, [(i, i ^ step) for i in range(size)])]
    ppermute x0 -> x7, waiting for transfers between devices: none -> 6.45 us  [pairwise_exchange(): lax.ppermute(sent, axis, [(i, i ^ step) for i in range(size)])]
    another operation x0 -> x2, local copies, waits for them, and re-layouts: none -> 5.92 us  [the longest x1 5.21 us: pairwise_exchange(): pieces = jnp.stack(finished)[here ^ jnp.arange(size)]]
  transfers between devices with their start and end apart: 3 -> 10, of which waited for: 2 -> 5; matrix products, arithmetic and copies ran while one was open for 3% -> 5% of each run, Pallas kernels for 0% -> 0%
where the time goes in v1:
time: 250 us; the launch traced here: 249 us
  waiting for transfers between devices  86.8 us (35%)
  local copies, waits for them, and re-layouts  54.6 us (22%)
  matrix products  48.9 us (20%)
  other arithmetic  28.3 us (11%)
  starting transfers between devices  16.1 us (6%)
  between operations  13.6 us (5%)
    all_gather x1, waiting for transfers between devices, body(): lax.all_gather(fetched, 'gz', axis=1, tiled=True)  57.2 us
    dot_general x8, matrix products, attend_block(): jnp.dot(flat_queries, key_sets.T, preferred_element_type=jnp.float32)  32.8 us
    all_to_all x1, waiting for transfers between devices, body(): lax.all_to_all(outgoing, ('gx', 'gy'), split_axis=0, concat_axis=0, tiled...  23 us
    squeeze x16, local copies, waits for them, and re-layouts, body(): return lax.map(one_block, (queries, own_blocks, pair_blocks, live_pairs))  19.1 us
    dot_general x8, matrix products, attend_block(): jnp.dot(weights.astype(jnp.bfloat16), value_sets, preferred_element_type=...  16.1 us
    reduce_sum x8, other arithmetic, attend_block(): row_total = jnp.sum(weights, axis=1, keepdims=True)  14.8 us
    ppermute x7, starting transfers between devices, pairwise_exchange(): lax.ppermute(sent, axis, [(i, i ^ step) for i in range(size)])  12.5 us
    gt x8, other arithmetic, allowed_mask(): far_part = (key_pos >= block_len) & (live_pair[pair_slot] > 0)  10.2 us
  transfers between devices with their start and end apart: 10, of which 5 were waited for; matrix products, arithmetic and copies ran while one was open for 5% of the time, Pallas kernels for 0%

profile of v1, /device:TPU:0, one launch (start us, length us, event | category | flops | bytes accessed | tf_op | source)
XLA Modules:
  0.0 248.7 jit_solution(170155633899455180)
XLA Ops:
  11.1 3.0 %collective-permute-start = (s32[1,1]{1,0:T(1,128)}, s32[1,1]{1,0:T(1,128)}, u32[]{:S(2)}, u32[]{:S(2)}) collective-permute-start(s32[1,1]{1,0:T(1,128)} %bitcast.9), channel_id=1, source_target_pairs={{0,4},{4,0},{8,12},{12,8},{16,20},{20,16},{24,28},{28,24},{1,5},{5... | collective-permute-start | bytes 20 | tf_op jit(solution)/shard_map/ppermute | solution.py:26
  14.1 1.6 collective-permute-start.1
  15.7 3.0 %collective-permute-start.3 = (s32[1,1]{1,0:T(1,128)}, s32[1,1]{1,0:T(1,128)}, u32[]{:S(2)}, u32[]{:S(2)}) collective-permute-start(s32[1,1]{1,0:T(1,128)} %bitcast.15), channel_id=1, source_target_pairs={{0,16},{4,20},{8,24},{12,28},{16,0},{20,4},{24,8},{28,12},{1,17},{... | collective-permute-start | bytes 20 | tf_op jit(solution)/shard_map/ppermute | solution.py:26
  20.0 3.7 %collective-permute-start.5 = (s32[1,1]{1,0:T(1,128)}, s32[1,1]{1,0:T(1,128)}, u32[]{:S(2)}, u32[]{:S(2)}) collective-permute-start(s32[1,1]{1,0:T(1,128)} %bitcast.19), channel_id=1, source_target_pairs={{0,24},{4,28},{8,16},{12,20},{16,8},{20,12},{24,0},{28,4},{1,25},{... | collective-permute-start | bytes 20 | tf_op jit(solution)/shard_map/ppermute | solution.py:26
  25.6 4.6 %collective-permute-done.6 = s32[1,1]{1,0:T(1,128)} collective-permute-done((s32[1,1]{1,0:T(1,128)}, s32[1,1]{1,0:T(1,128)}, u32[]{:S(2)}, u32[]{:S(2)}) %collective-permute-start.6) | collective-permute-done | bytes 36 | tf_op jit(solution)/shard_map/ppermute | solution.py:26
  30.1 5.2 %stack.31 = s32[8,1,1]{0,2,1:T(1,128)S(1)} concatenate(s32[1,1,1]{0,2,1:T(1,128)} %bitcast.8, s32[1,1,1]{0,2,1:T(1,128)} %bitcast.10, s32[1,1,1]{0,2,1:T(1,128)} %bitcast.12, s32[1,1,1]{0,2,1:T(1,128)} %bitcast.14, s32[1,1,1]{0,2,1:T(1,128)} %bitcast.16, s32[1,1,1]{0,2,1:T(1,128)} %bitcast.18, s32[1,1,1]{0,2,1:T(1,128)} %bitcast.20, s32[1,1,1]{0,2,1:T(1,128)} %bitcast.22), dimensions={0} | concatenate | bytes 64 | tf_op jit(solution)/shard_map/stack | solution.py:27
  36.0 1.8 gather_fusion.1
  39.0 3.6 %all-to-all-start = ((bf16[8,1,256,256]{3,2,1,0:T(8,128)(2,1)}), bf16[8,1,256,256]{3,2,1,0:T(8,128)(2,1)S(1)}, u32[]{:S(2)}, u32[]{:S(2)}) async-start(bf16[8,1,256,256]{3,2,1,0:T(8,128)(2,1)} %bitcast_select_fusion), calls=%async_computation | async-start | bytes 2097152 | tf_op jit(solution)/shard_map/all_to_all | solution.py:81
  42.7 23.0 %all-to-all-done = bf16[8,1,256,256]{3,2,1,0:T(8,128)(2,1)S(1)} async-done(((bf16[8,1,256,256]{3,2,1,0:T(8,128)(2,1)}), bf16[8,1,256,256]{3,2,1,0:T(8,128)(2,1)S(1)}, u32[]{:S(2)}, u32[]{:S(2)}) %all-to-all-start) | async-done | bytes 1048608 | tf_op jit(solution)/shard_map/all_to_all | solution.py:81
  66.4 1.6 broadcast_select_fusion
  68.1 57.2 %all-gather.5.cloned.1.call-done = bf16[16,1024,256]{2,1,0:T(8,128)(2,1)} async-done(((bf16[16,256,256]{2,1,0:T(8,128)(2,1)}), bf16[16,1024,256]{2,1,0:T(8,128)(2,1)}) %all-gather.5.cloned.1.call-update) | async-done | bytes 8388624 | tf_op jit(solution)/shard_map/all_gather | solution.py:86
  125.3 116.5 %while.13 = (s32[]{:T(128)}, bf16[8,256,512]{2,1,0:T(8,128)(2,1)}, s32[]{:T(128)}, s32[8,2]{0,1:T(2,128)S(1)}, bf16[8,256,512]{2,1,0:T(8,128)(2,1)}, /*index=5*/...) while((s32[]{:T(128)}, bf16[8,256,512]{2,1,0:T(8,128)(2,1)}, s32[]{:T(128)}, ...), condition=%wide.region_5.6_spmd, body=%wide.region_2.5_spmd.sunk | while | flops 1647116288 | bytes 48282256 | solution.py:104
  126.0 1.3 compare_reduce_fusion.2
  127.2 1.3 dynamic-slice_bitcast_fusion.4
  131.0 4.1 %fusion.59 = (f32[1024]{0:T(1024)S(1)}, f32[1024,3072]{1,0:T(8,128)S(1)}) fusion(bf16[1024,128]{1,0:T(8,128)(2,1)S(1)} %reshape.574, bf16[1024,128]{1,0:T(8,128)(2,1)S(1)} %get-tuple-element.219, bf16[1024,128]{1,0:T(8,128)(2,1)S(1)} %get-tuple-element.220, bf16[1024,128]{1,0:T(8,128)(2,1)S(1)} %get-tuple-element.221, ...), kind=kOutput, calls=%fused_computation.95.clone.1 | convolution fusion | flops 826539008 | bytes 13645824 | tf_op jit(solution)/shard_map/while/body/eval_jaxpr/dot_general | solution.py:43
  135.1 1.9 fusion.60
  137.0 2.0 fusion.61
  140.5 1.3 compare_reduce_fusion.2
  141.8 1.3 dynamic-slice_bitcast_fusion.4
  145.6 4.1 %fusion.59 = (f32[1024]{0:T(1024)S(1)}, f32[1024,3072]{1,0:T(8,128)S(1)}) fusion(bf16[1024,128]{1,0:T(8,128)(2,1)S(1)} %reshape.574, bf16[1024,128]{1,0:T(8,128)(2,1)S(1)} %get-tuple-element.219, bf16[1024,128]{1,0:T(8,128)(2,1)S(1)} %get-tuple-element.220, bf16[1024,128]{1,0:T(8,128)(2,1)S(1)} %get-tuple-element.221, ...), kind=kOutput, calls=%fused_computation.95.clone.1 | convolution fusion | flops 826539008 | bytes 13645824 | tf_op jit(solution)/shard_map/while/body/eval_jaxpr/dot_general | solution.py:43
  149.7 1.9 fusion.60
  151.5 2.0 fusion.61
  155.1 1.3 compare_reduce_fusion.2
  156.4 1.3 dynamic-slice_bitcast_fusion.4
  160.2 4.1 %fusion.59 = (f32[1024]{0:T(1024)S(1)}, f32[1024,3072]{1,0:T(8,128)S(1)}) fusion(bf16[1024,128]{1,0:T(8,128)(2,1)S(1)} %reshape.574, bf16[1024,128]{1,0:T(8,128)(2,1)S(1)} %get-tuple-element.219, bf16[1024,128]{1,0:T(8,128)(2,1)S(1)} %get-tuple-element.220, bf16[1024,128]{1,0:T(8,128)(2,1)S(1)} %get-tuple-element.221, ...), kind=kOutput, calls=%fused_computation.95.clone.1 | convolution fusion | flops 826539008 | bytes 13645824 | tf_op jit(solution)/shard_map/while/body/eval_jaxpr/dot_general | solution.py:43
  164.3 1.9 fusion.60
  166.1 2.0 fusion.61
  169.6 1.3 compare_reduce_fusion.2
  170.9 1.3 dynamic-slice_bitcast_fusion.4
  174.7 4.1 %fusion.59 = (f32[1024]{0:T(1024)S(1)}, f32[1024,3072]{1,0:T(8,128)S(1)}) fusion(bf16[1024,128]{1,0:T(8,128)(2,1)S(1)} %reshape.574, bf16[1024,128]{1,0:T(8,128)(2,1)S(1)} %get-tuple-element.219, bf16[1024,128]{1,0:T(8,128)(2,1)S(1)} %get-tuple-element.220, bf16[1024,128]{1,0:T(8,128)(2,1)S(1)} %get-tuple-element.221, ...), kind=kOutput, calls=%fused_computation.95.clone.1 | convolution fusion | flops 826539008 | bytes 13645824 | tf_op jit(solution)/shard_map/while/body/eval_jaxpr/dot_general | solution.py:43
  178.8 1.9 fusion.60
  180.7 2.0 fusion.61
  185.5 1.3 dynamic-slice_bitcast_fusion.4
  189.3 4.1 %fusion.59 = (f32[1024]{0:T(1024)S(1)}, f32[1024,3072]{1,0:T(8,128)S(1)}) fusion(bf16[1024,128]{1,0:T(8,128)(2,1)S(1)} %reshape.574, bf16[1024,128]{1,0:T(8,128)(2,1)S(1)} %get-tuple-element.219, bf16[1024,128]{1,0:T(8,128)(2,1)S(1)} %get-tuple-element.220, bf16[1024,128]{1,0:T(8,128)(2,1)S(1)} %get-tuple-element.221, ...), kind=kOutput, calls=%fused_computation.95.clone.1 | convolution fusion | flops 826539008 | bytes 13645824 | tf_op jit(solution)/shard_map/while/body/eval_jaxpr/dot_general | solution.py:43
  193.4 1.9 fusion.60
  195.3 2.0 fusion.61
  200.1 1.3 dynamic-slice_bitcast_fusion.4
  203.9 4.1 %fusion.59 = (f32[1024]{0:T(1024)S(1)}, f32[1024,3072]{1,0:T(8,128)S(1)}) fusion(bf16[1024,128]{1,0:T(8,128)(2,1)S(1)} %reshape.574, bf16[1024,128]{1,0:T(8,128)(2,1)S(1)} %get-tuple-element.219, bf16[1024,128]{1,0:T(8,128)(2,1)S(1)} %get-tuple-element.220, bf16[1024,128]{1,0:T(8,128)(2,1)S(1)} %get-tuple-element.221, ...), kind=kOutput, calls=%fused_computation.95.clone.1 | convolution fusion | flops 826539008 | bytes 13645824 | tf_op jit(solution)/shard_map/while/body/eval_jaxpr/dot_general | solution.py:43
  208.0 1.9 fusion.60
  209.8 2.0 fusion.61
  214.6 1.3 dynamic-slice_bitcast_fusion.4
  218.4 4.1 %fusion.59 = (f32[1024]{0:T(1024)S(1)}, f32[1024,3072]{1,0:T(8,128)S(1)}) fusion(bf16[1024,128]{1,0:T(8,128)(2,1)S(1)} %reshape.574, bf16[1024,128]{1,0:T(8,128)(2,1)S(1)} %get-tuple-element.219, bf16[1024,128]{1,0:T(8,128)(2,1)S(1)} %get-tuple-element.220, bf16[1024,128]{1,0:T(8,128)(2,1)S(1)} %get-tuple-element.221, ...), kind=kOutput, calls=%fused_computation.95.clone.1 | convolution fusion | flops 826539008 | bytes 13645824 | tf_op jit(solution)/shard_map/while/body/eval_jaxpr/dot_general | solution.py:43
  222.5 1.9 fusion.60
  224.4 2.0 fusion.61
  229.2 1.3 dynamic-slice_bitcast_fusion.4
  233.0 4.1 %fusion.59 = (f32[1024]{0:T(1024)S(1)}, f32[1024,3072]{1,0:T(8,128)S(1)}) fusion(bf16[1024,128]{1,0:T(8,128)(2,1)S(1)} %reshape.574, bf16[1024,128]{1,0:T(8,128)(2,1)S(1)} %get-tuple-element.219, bf16[1024,128]{1,0:T(8,128)(2,1)S(1)} %get-tuple-element.220, bf16[1024,128]{1,0:T(8,128)(2,1)S(1)} %get-tuple-element.221, ...), kind=kOutput, calls=%fused_computation.95.clone.1 | convolution fusion | flops 826539008 | bytes 13645824 | tf_op jit(solution)/shard_map/while/body/eval_jaxpr/dot_general | solution.py:43
  237.1 1.9 fusion.60
  239.0 2.0 fusion.61
  (133 shorter events, 47.1 us)
Async XLA Ops:
  6.5 3.4 %copy-start.1 = (s32[8,2]{0,1:T(2,128)S(1)}, s32[8,2]{0,1:T(2,128)}, u32[]{:S(2)}) copy-start(s32[8,2]{0,1:T(2,128)} %param.9) | copy-start | bytes 196
  6.5 61.6 %all-gather.3.cloned.1.call-start = ((), (), s32[]{:S(2)}) async-start(), calls=%async_computation.1 | async-start | bytes 5242880 | tf_op jit(solution)/shard_map/all_gather | solution.py:87
  8.9 1.0 copy-start
  11.1 8.8 %collective-permute-start = (s32[1,1]{1,0:T(1,128)}, s32[1,1]{1,0:T(1,128)}, u32[]{:S(2)}, u32[]{:S(2)}) collective-permute-start(s32[1,1]{1,0:T(1,128)} %bitcast.9), channel_id=1, source_target_pairs={{0,4},{4,0},{8,12},{12,8},{16,20},{20,16},{24,28},{28,24},{1,5},{5... | collective-permute-start | bytes 20 | tf_op jit(solution)/shard_map/ppermute | solution.py:26
  14.1 9.5 %collective-permute-start.1 = (s32[1,1]{1,0:T(1,128)}, s32[1,1]{1,0:T(1,128)}, u32[]{:S(2)}, u32[]{:S(2)}) collective-permute-start(s32[1,1]{1,0:T(1,128)} %bitcast.11), channel_id=1, source_target_pairs={{0,8},{4,12},{8,0},{12,4},{16,24},{20,28},{24,16},{28,20},{1,9},{5... | collective-permute-start | bytes 20 | tf_op jit(solution)/shard_map/ppermute | solution.py:26
  15.7 8.0 %collective-permute-start.2 = (s32[1,1]{1,0:T(1,128)}, s32[1,1]{1,0:T(1,128)}, u32[]{:S(2)}, u32[]{:S(2)}) collective-permute-start(s32[1,1]{1,0:T(1,128)} %bitcast.13), channel_id=1, source_target_pairs={{0,12},{4,8},{8,4},{12,0},{16,28},{20,24},{24,20},{28,16},{1,13},{... | collective-permute-start | bytes 20 | tf_op jit(solution)/shard_map/ppermute | solution.py:26
  15.7 8.0 %collective-permute-start.3 = (s32[1,1]{1,0:T(1,128)}, s32[1,1]{1,0:T(1,128)}, u32[]{:S(2)}, u32[]{:S(2)}) collective-permute-start(s32[1,1]{1,0:T(1,128)} %bitcast.15), channel_id=1, source_target_pairs={{0,16},{4,20},{8,24},{12,28},{16,0},{20,4},{24,8},{28,12},{1,17},{... | collective-permute-start | bytes 20 | tf_op jit(solution)/shard_map/ppermute | solution.py:26
  18.7 5.7 %collective-permute-start.4 = (s32[1,1]{1,0:T(1,128)}, s32[1,1]{1,0:T(1,128)}, u32[]{:S(2)}, u32[]{:S(2)}) collective-permute-start(s32[1,1]{1,0:T(1,128)} %bitcast.17), channel_id=1, source_target_pairs={{0,20},{4,16},{8,28},{12,24},{16,4},{20,0},{24,12},{28,8},{1,21},{... | collective-permute-start | bytes 20 | tf_op jit(solution)/shard_map/ppermute | solution.py:26
  20.0 5.6 %collective-permute-start.5 = (s32[1,1]{1,0:T(1,128)}, s32[1,1]{1,0:T(1,128)}, u32[]{:S(2)}, u32[]{:S(2)}) collective-permute-start(s32[1,1]{1,0:T(1,128)} %bitcast.19), channel_id=1, source_target_pairs={{0,24},{4,28},{8,16},{12,20},{16,8},{20,12},{24,0},{28,4},{1,25},{... | collective-permute-start | bytes 20 | tf_op jit(solution)/shard_map/ppermute | solution.py:26
  23.6 6.5 %collective-permute-start.6 = (s32[1,1]{1,0:T(1,128)}, s32[1,1]{1,0:T(1,128)}, u32[]{:S(2)}, u32[]{:S(2)}) collective-permute-start(s32[1,1]{1,0:T(1,128)} %bitcast.21), channel_id=1, source_target_pairs={{0,28},{4,24},{8,20},{12,16},{16,12},{20,8},{24,4},{28,0},{1,29},{... | collective-permute-start | bytes 20 | tf_op jit(solution)/shard_map/ppermute | solution.py:26
  39.0 26.7 %all-to-all-start = ((bf16[8,1,256,256]{3,2,1,0:T(8,128)(2,1)}), bf16[8,1,256,256]{3,2,1,0:T(8,128)(2,1)S(1)}, u32[]{:S(2)}, u32[]{:S(2)}) async-start(bf16[8,1,256,256]{3,2,1,0:T(8,128)(2,1)} %bitcast_select_fusion), calls=%async_computation | async-start | bytes 2097152 | tf_op jit(solution)/shard_map/all_to_all | solution.py:81
  42.6 82.8 %all-gather.5.cloned.1.call-start = ((), (), s32[]{:S(2)}) async-start(), calls=%async_computation.2 | async-start | bytes 10485760 | tf_op jit(solution)/shard_map/all_gather | solution.py:86
Sparse Core Ops, SparseCore 0:
  10.0 37.1 all-gather.2
  68.2 57.1 all-gather.4
